TPU v7x, 32 devices: a whole 2x2x4 slice. The times are simulated.
32 devices in a mesh: col: 8 (over y, x, core), dev: 4 (over z).
Axes of the slice: x: 2, y: 2, z: 4, core: 2. Of those that a mesh axis runs over, the one named last changes fastest.
Arguments:
- first_factor: bfloat16 [16, 1024, 2048], P(None, 'col', 'dev'), may hold values from -1 to 1
- second_factor: bfloat16 [16, 1024, 2048], P(None, 'dev', 'col'), may hold values from -1 to 1
- amplitudes: bfloat16 [512, 1024, 1024], P(None, 'col', 'dev'), may hold values from -0.0059814453 to 0.0059814453
Outputs:
- ladder: float32 [512, 256], P(('col', 'dev'))
All inputs are finite; a program needn't handle non-finite values.
Results may differ from a plain program's by a relative error of at most 0.0029.
Values may be sent and summed in bfloat16 or wider, within the bound.
A program may use at most 128 MiB of HBM per device.

v0:
```python
import functools

import jax
import jax.numpy as jnp
from jax import lax
from jax.experimental import pallas as pl
from jax.experimental.pallas import tpu as pltpu
from jax.sharding import PartitionSpec as P

MESH = pl.DeviceIdType.MESH
CHUNKS = 8
AHEAD = 2
GROUP = 8
WIDE = 8
NT = (((1,), (1,)), ((), ()))


def kernel(
    ncol, ndev, first, second, amps, out,
    first_all, second_all, raw, turned, tile, total, parts, final, half_sum,
    own_sem, z_send, z_recv, r_send, r_recv, c_send, c_recv, t_sem, s_send, s_recv, d_send, d_recv,
):
    col, dev = lax.axis_index("col"), lax.axis_index("dev")
    n_c, n_a, q_first = first.shape
    n_b, n_d, q_second = second.shape
    pairs = amps.shape[0]
    size = n_c // CHUNKS
    chips = ncol // 2
    far = chips // 2
    core, chip = lax.rem(col, 2), col // 2

    def swap(spot):
        return jnp.where(spot < far, spot, 3 * far - 1 - spot)

    spot = swap(chip)

    def at_spot(offset):
        return swap(lax.rem(spot + offset + 2 * chips, chips)) * 2 + core

    partner = chip * 2 + 1 - core

    barrier = pltpu.get_barrier_semaphore()
    for off in range(1, ncol):
        pl.semaphore_signal(
            barrier, inc=1, device_id={"col": lax.rem(col + off, ncol)}, device_id_type=MESH
        )
    for off in range(1, ndev):
        pl.semaphore_signal(
            barrier, inc=1, device_id={"dev": lax.rem(dev + off, ndev)}, device_id_type=MESH
        )
    pl.semaphore_wait(barrier, ncol + ndev - 2)

    def z_slice(source, k):
        return first_all.at[
            pl.ds(k * size, size), :, pl.ds(pl.multiple_of(source * q_first, q_first), q_first)
        ]

    def z_copy(way, hop, k):
        step = 1 if way == 0 else -1
        source = dev - step * (hop - 1)
        src = first.at[pl.ds(k * size, size)] if hop == 1 else z_slice(source, k)
        return pltpu.make_async_remote_copy(
            src_ref=src,
            dst_ref=z_slice(source, k),
            send_sem=z_send.at[way, hop - 1, k],
            recv_sem=z_recv.at[way, hop - 1, k],
            device_id={"dev": dev + step},
            device_id_type=MESH,
        )

    def z_arrival(way, hop, k):
        step = 1 if way == 0 else -1
        here = z_slice(dev - step * hop, k)
        return pltpu.make_async_copy(here, here, z_recv.at[way, hop - 1, k])

    def sends(way, hop):
        if way == 0:
            return (dev - (hop - 1) >= 0) & (dev + 1 < ndev)
        return (dev + (hop - 1) < ndev) & (dev - 1 >= 0)

    def receives(way, hop):
        return (dev - hop >= 0) if way == 0 else (dev + hop < ndev)

    def z_own(k):
        for way in range(2):
            @pl.when(sends(way, 1))
            def _():
                z_copy(way, 1, k).start()

    def z_round(k):
        @pl.when(k + AHEAD < CHUNKS)
        def _():
            z_own(k + AHEAD)

        for hop in range(1, ndev):
            for way in range(2):
                @pl.when(receives(way, hop))
                def _():
                    z_arrival(way, hop, k).wait()

                if hop + 1 < ndev:
                    @pl.when(sends(way, hop + 1))
                    def _():
                        z_copy(way, hop + 1, k).start()

    wide = n_b // 2

    def p_slice(source, h):
        return second_all.at[
            pl.ds(h * wide, wide), :, pl.ds(pl.multiple_of(source * q_second, q_second), q_second)
        ]

    def p_source(way, hop):
        return at_spot(-hop if way == 0 else hop)

    def r_copy(way, hop, h):
        source = p_source(way, hop - 1)
        src = second.at[pl.ds(h * wide, wide)] if hop == 1 else p_slice(source, h)
        return pltpu.make_async_remote_copy(
            src_ref=src,
            dst_ref=p_slice(source, h),
            send_sem=r_send.at[way, hop - 1, h],
            recv_sem=r_recv.at[way, hop - 1, h],
            device_id={"col": at_spot(1 if way == 0 else -1)},
            device_id_type=MESH,
        )

    def r_arrival(way, hop, h):
        here = p_slice(p_source(way, hop), h)
        return pltpu.make_async_copy(here, here, r_recv.at[way, hop - 1, h])

    def c_copy(way, hop, h):
        source = p_source(way, hop)
        src = second.at[pl.ds(h * wide, wide)] if hop == 0 else p_slice(source, h)
        return pltpu.make_async_remote_copy(
            src_ref=src,
            dst_ref=p_slice(source, h),
            send_sem=c_send.at[way, hop, h],
            recv_sem=c_recv.at[way, hop, h],
            device_id={"col": partner},
            device_id_type=MESH,
        )

    def c_arrival(way, hop, h):
        source = p_source(way, hop) + 1 - 2 * core
        here = p_slice(source, h)
        return pltpu.make_async_copy(here, here, c_recv.at[way, hop, h])

    def travels(way, hop):
        if hop < far:
            return (0, 1) if way == 0 else (1, 0)
        return (way,) if hop == far else ()

    pieces = [
        (way, hop, travels(way, hop)[place])
        for hop in range(1, far + 1)
        for place in range(len(travels(0, hop)))
        for way in range(2)
    ]
    shared = [(0, 0, 0), (0, 0, 1)] + pieces

    own_first = pltpu.make_async_copy(
        first, first_all.at[:, :, pl.ds(pl.multiple_of(dev * q_first, q_first), q_first)],
        own_sem.at[0],
    )
    own_second = pltpu.make_async_copy(
        second, second_all.at[:, :, pl.ds(pl.multiple_of(col * q_second, q_second), q_second)],
        own_sem.at[1],
    )

    def t_copy(k):
        slot = lax.rem(k, 2)
        return pltpu.make_async_copy(
            amps.at[:, pl.ds(pl.multiple_of(k * size, size), size), :], raw.at[slot],
            t_sem.at[slot],
        )

    for k in range(AHEAD):
        z_own(k)
    for way, hop, h in pieces:
        if hop == 1:
            r_copy(way, 1, h).start()
    own_first.start()
    own_second.start()
    t_copy(0).start()
    for h in range(2):
        c_copy(0, 0, h).start()

    lead = CHUNKS // 2
    by_round = [[] for _ in range(lead)]
    for number, piece in enumerate(pieces):
        by_round[min(lead - 1, 1 + number * lead // len(pieces))].append(piece)

    def take(way, hop, h):
        r_arrival(way, hop, h).wait()
        if h in travels(way, hop + 1):
            r_copy(way, hop + 1, h).start()
        c_copy(way, hop, h).start()

    def turn_block(k):
        slot, held = lax.rem(k, 2), lax.rem(k, lead)
        t_copy(k).wait()

        @pl.when(k + 1 < CHUNKS)
        def _():
            t_copy(k + 1).start()

        def turn(i, _):
            rows = pl.ds(pl.multiple_of(i * 16, 16), 16)
            turned[held, :, rows, :] = jnp.swapaxes(raw[slot, rows], 0, 1)
            return 0

        lax.fori_loop(0, pairs // 16, turn, 0)

    for k in range(lead):
        turn_block(k)
        for piece in by_round[k]:
            take(*piece)
        z_round(k)
    own_first.wait()
    own_second.wait()
    for piece in shared:
        c_arrival(*piece).wait()

    total[...] = jnp.zeros_like(total)

    def one_block(k, _):
        held = lax.rem(k, lead)

        def one_b(b, _):
            left = first_all[pl.ds(k * size, size)].reshape(size * n_a, -1)
            right = second_all[pl.ds(b * WIDE, WIDE)].reshape(WIDE * n_d, -1)
            got = lax.dot_general(left, right, NT, preferred_element_type=jnp.float32)
            got = got.astype(jnp.bfloat16)
            for i in range(WIDE):
                tile[:, b * WIDE + i] = got[:, i * n_d : (i + 1) * n_d].reshape(size, n_a, n_d)
            return 0

        lax.fori_loop(0, n_b // WIDE, one_b, 0)

        def some_c(g, _):
            group = [g * GROUP + i for i in range(GROUP)]
            left = jnp.concatenate([turned[held, c] for c in group], axis=1)
            right = jnp.concatenate([tile[c].reshape(n_b * n_a, n_d) for c in group], axis=1)
            total[...] += lax.dot_general(left, right, NT, preferred_element_type=jnp.float32)
            return 0

        lax.fori_loop(0, size // GROUP, some_c, 0)

        @pl.when(k + lead < CHUNKS)
        def _():
            turn_block(k + lead)

        @pl.when(((lax.rem(k, 2) == 1) & (k < CHUNKS - 1)) | (k == CHUNKS - 2))
        def _():
            z_round(lead + k // 2)

        return 0

    lax.fori_loop(0, CHUNKS, one_block, 0)

    some = pairs // ncol

    def s_copy(off):
        to = lax.rem(col + off, ncol)
        return pltpu.make_async_remote_copy(
            src_ref=total.at[pl.ds(pl.multiple_of(to * some, some), some)],
            dst_ref=parts.at[off],
            send_sem=s_send.at[off],
            recv_sem=s_recv.at[off],
            device_id={"col": to},
            device_id_type=MESH,
        )

    for off in range(1, ncol):
        s_copy(off).start()
    mine = total[pl.ds(pl.multiple_of(col * some, some), some), :]
    for off in range(1, ncol):
        s_copy(off).wait_recv()
        mine += parts[off]
    half_sum[...] = mine.reshape(half_sum.shape)

    def d_copy(off):
        to = lax.rem(dev + off, ndev)
        return pltpu.make_async_remote_copy(
            src_ref=half_sum.at[to],
            dst_ref=final.at[off],
            send_sem=d_send.at[off],
            recv_sem=d_recv.at[off],
            device_id={"dev": to},
            device_id_type=MESH,
        )

    for off in range(1, ndev):
        d_copy(off).start()
    result = half_sum[dev]
    for off in range(1, ndev):
        d_copy(off).wait_recv()
        result += final[off]
    out[...] = result

    for off in range(1, ncol):
        s_copy(off).wait_send()
    for off in range(1, ndev):
        d_copy(off).wait_send()
    for piece in pieces:
        r_copy(*piece).wait_send()
    for piece in shared:
        c_copy(*piece).wait_send()

    def drain(k, _):
        for way in range(2):
            for hop in range(1, ndev):
                @pl.when(sends(way, hop))
                def _():
                    z_copy(way, hop, k).wait_send()
        return 0

    lax.fori_loop(0, CHUNKS, drain, 0)


def on_device(ncol, ndev, first_factor, second_factor, amplitudes):
    n_a, n_c, q_first = first_factor.shape
    n_b, n_d, q_second = second_factor.shape
    pairs = amplitudes.shape[0]
    size = n_c // CHUNKS
    far = ncol // 4
    whole = q_first * ndev
    some = pairs // ncol
    few = some // ndev
    width = n_a * n_b
    anywhere = pl.BlockSpec(memory_space=pl.ANY)
    dma = pltpu.SemaphoreType.DMA
    got = pl.pallas_call(
        functools.partial(kernel, ncol, ndev),
        out_shape=jax.ShapeDtypeStruct((few, width), jnp.float32),
        in_specs=[anywhere] * 3,
        out_specs=pl.BlockSpec(memory_space=pltpu.VMEM),
        scratch_shapes=[
            pltpu.VMEM((n_c, n_a, whole), jnp.bfloat16),
            pltpu.VMEM((n_b, n_d, whole), jnp.bfloat16),
            pltpu.VMEM((2, pairs, size, n_d), jnp.bfloat16),
            pltpu.VMEM((CHUNKS // 2, size, pairs, n_d), jnp.bfloat16),
            pltpu.VMEM((size, n_b, n_a, n_d), jnp.bfloat16),
            pltpu.VMEM((pairs, width), jnp.float32),
            pltpu.VMEM((ncol, some, width), jnp.float32),
            pltpu.VMEM((ndev, few, width), jnp.float32),
            pltpu.VMEM((ndev, few, width), jnp.float32),
            dma((2,)),
            dma((2, ndev - 1, CHUNKS)),
            dma((2, ndev - 1, CHUNKS)),
            dma((2, far, 2)),
            dma((2, far, 2)),
            dma((2, far + 1, 2)),
            dma((2, far + 1, 2)),
            dma((2,)),
            dma((ncol,)),
            dma((ncol,)),
            dma((ndev,)),
            dma((ndev,)),
        ],
        compiler_params=pltpu.CompilerParams(
            collective_id=0, has_side_effects=True, vmem_limit_bytes=58 * 2**20
        ),
    )(jnp.swapaxes(first_factor, 0, 1), second_factor, amplitudes)
    return jnp.swapaxes(got.reshape(few, n_b, n_a), 1, 2).reshape(few, width)


def solution(mesh):
    placed = (P(None, "col", "dev"), P(None, "dev", "col"), P(None, "col", "dev"))
    return jax.shard_map(
        functools.partial(on_device, mesh.shape["col"], mesh.shape["dev"]),
        mesh=mesh, in_specs=placed, out_specs=P(("col", "dev"), None), check_vma=False,
    )
```

profile of v0, /device:TPU:0, one launch (start us, length us, event | category | flops | bytes accessed | tf_op | source)
XLA Modules:
  0.0 198.3 jit_solution(6634421963073187282)
XLA Ops:
  0.0 4.1 %copy.7 = bf16[16,128,512]{2,0,1:T(8,128)(2,1)} copy(bf16[16,128,512]{2,1,0:T(8,128)(2,1)} %param.3) | data formatting | bytes 4194304 | tf_op args[0]
  4.1 192.5 %shard_map.37 = f32[16,256]{1,0:T(8,128)} custom-call(bf16[128,16,512]{2,1,0:T(8,128)(2,1)} %bitcast.4, bf16[16,256,256]{2,1,0:T(8,128)(2,1)} %second.1, bf16[512,128,256]{2,1,0:T(8,128)(2,1)} %amps.1), custom_call_target="tpu_custom_call" | custom-call | tf_op jit(solution)/shard_map/pallas_call | solution.py:334
  196.7 0.8 reshape.6
  197.5 0.1 copy.5
  197.6 0.7 reshape.7
where the time goes:
time: 199 us; the launch traced here: 198 us
  Pallas kernels  193 us (97%)
  local copies, waits for them, and re-layouts  5.72 us (3%)
    pallas_call x1, Pallas kernels, on_device(): pl.pallas_call(functools.partial(kernel, ncol, ndev), out_shape=jax.Shape...  193 us
    unnamed x1, local copies, waits for them, and re-layouts  4.1 us

commit v1 on v0

--- a/solution.py
+++ b/solution.py
@@ -8,23 +8,25 @@
 from jax.sharding import PartitionSpec as P
 
 MESH = pl.DeviceIdType.MESH
-CHUNKS = 8
-AHEAD = 2
+BLOCK = 16
 GROUP = 8
 WIDE = 8
+EARLY = 3
 NT = (((1,), (1,)), ((), ()))
 
 
 def kernel(
     ncol, ndev, first, second, amps, out,
-    first_all, second_all, raw, turned, tile, total, parts, final, half_sum,
-    own_sem, z_send, z_recv, r_send, r_recv, c_send, c_recv, t_sem, s_send, s_recv, d_send, d_recv,
+    first_all, second_all, held, tile, total, parts, final, half_sum,
+    f_sem, own_sem, z_send, z_recv, r_send, r_recv, c_send, c_recv, t_sem, s_send, s_recv, d_send, d_recv,
 ):
     col, dev = lax.axis_index("col"), lax.axis_index("dev")
-    n_c, n_a, q_first = first.shape
+    n_a, n_c, q_first = first.shape
     n_b, n_d, q_second = second.shape
-    pairs = amps.shape[0]
-    size = n_c // CHUNKS
+    groups = amps.shape[0]
+    pairs = groups * BLOCK
+    size = n_a
+    chunks = n_c // size
     chips = ncol // 2
     far = chips // 2
     core, chip = lax.rem(col, 2), col // 2
@@ -38,6 +40,7 @@
         return swap(lax.rem(spot + offset + 2 * chips, chips)) * 2 + core
 
     partner = chip * 2 + 1 - core
+    own_q = pl.ds(pl.multiple_of(dev * q_first, q_first), q_first)
 
     barrier = pltpu.get_barrier_semaphore()
     for off in range(1, ncol):
@@ -48,7 +51,24 @@
         pl.semaphore_signal(
             barrier, inc=1, device_id={"dev": lax.rem(dev + off, ndev)}, device_id_type=MESH
         )
-    pl.semaphore_wait(barrier, ncol + ndev - 2)
+
+    def f_copy(k):
+        return pltpu.make_async_copy(
+            first.at[:, pl.ds(pl.multiple_of(k * size, size), size), :],
+            first_all.at[pl.ds(k * size, size), :, own_q],
+            f_sem.at[k],
+        )
+
+    def t_copy(k):
+        return pltpu.make_async_copy(
+            amps.at[:, :, pl.ds(pl.multiple_of(k * BLOCK, BLOCK), BLOCK), :], held.at[k],
+            t_sem.at[k],
+        )
+
+    own_second = pltpu.make_async_copy(
+        second, second_all.at[:, :, pl.ds(pl.multiple_of(col * q_second, q_second), q_second)],
+        own_sem.at[0],
+    )
 
     def z_slice(source, k):
         return first_all.at[
@@ -57,11 +77,10 @@
 
     def z_copy(way, hop, k):
         step = 1 if way == 0 else -1
-        source = dev - step * (hop - 1)
-        src = first.at[pl.ds(k * size, size)] if hop == 1 else z_slice(source, k)
-        return pltpu.make_async_remote_copy(
-            src_ref=src,
-            dst_ref=z_slice(source, k),
+        here = z_slice(dev - step * (hop - 1), k)
+        return pltpu.make_async_remote_copy(
+            src_ref=here,
+            dst_ref=here,
             send_sem=z_send.at[way, hop - 1, k],
             recv_sem=z_recv.at[way, hop - 1, k],
             device_id={"dev": dev + step},
@@ -87,21 +106,23 @@
             def _():
                 z_copy(way, 1, k).start()
 
-    def z_round(k):
-        @pl.when(k + AHEAD < CHUNKS)
-        def _():
-            z_own(k + AHEAD)
-
-        for hop in range(1, ndev):
-            for way in range(2):
-                @pl.when(receives(way, hop))
+    def z_relay(hop, k):
+        for way in range(2):
+            @pl.when(receives(way, hop) & sends(way, hop + 1))
+            def _():
+                z_arrival(way, hop, k).wait()
+                z_copy(way, hop + 1, k).start()
+
+    def z_need(k):
+        for way in range(2):
+            for hop in range(1, ndev):
+                kept = receives(way, hop)
+                if hop + 1 < ndev:
+                    kept &= jnp.logical_not(sends(way, hop + 1))
+
+                @pl.when(kept)
                 def _():
                     z_arrival(way, hop, k).wait()
-
-                if hop + 1 < ndev:
-                    @pl.when(sends(way, hop + 1))
-                    def _():
-                        z_copy(way, hop + 1, k).start()
 
     wide = n_b // 2
 
@@ -159,65 +180,57 @@
     ]
     shared = [(0, 0, 0), (0, 0, 1)] + pieces
 
-    own_first = pltpu.make_async_copy(
-        first, first_all.at[:, :, pl.ds(pl.multiple_of(dev * q_first, q_first), q_first)],
-        own_sem.at[0],
-    )
-    own_second = pltpu.make_async_copy(
-        second, second_all.at[:, :, pl.ds(pl.multiple_of(col * q_second, q_second), q_second)],
-        own_sem.at[1],
-    )
-
-    def t_copy(k):
-        slot = lax.rem(k, 2)
-        return pltpu.make_async_copy(
-            amps.at[:, pl.ds(pl.multiple_of(k * size, size), size), :], raw.at[slot],
-            t_sem.at[slot],
-        )
-
-    for k in range(AHEAD):
-        z_own(k)
-    for way, hop, h in pieces:
-        if hop == 1:
-            r_copy(way, 1, h).start()
-    own_first.start()
-    own_second.start()
-    t_copy(0).start()
-    for h in range(2):
-        c_copy(0, 0, h).start()
-
-    lead = CHUNKS // 2
-    by_round = [[] for _ in range(lead)]
-    for number, piece in enumerate(pieces):
-        by_round[min(lead - 1, 1 + number * lead // len(pieces))].append(piece)
-
     def take(way, hop, h):
         r_arrival(way, hop, h).wait()
         if h in travels(way, hop + 1):
             r_copy(way, hop + 1, h).start()
         c_copy(way, hop, h).start()
 
+    def turn_first(k):
+        f_copy(k).wait()
+        rows = pl.ds(k * size, size)
+        first_all[rows, :, own_q] = jnp.swapaxes(first_all[rows, :, own_q], 0, 1)
+
     def turn_block(k):
-        slot, held = lax.rem(k, 2), lax.rem(k, lead)
         t_copy(k).wait()
 
-        @pl.when(k + 1 < CHUNKS)
-        def _():
-            t_copy(k + 1).start()
-
         def turn(i, _):
-            rows = pl.ds(pl.multiple_of(i * 16, 16), 16)
-            turned[held, :, rows, :] = jnp.swapaxes(raw[slot, rows], 0, 1)
+            held[k, i] = jnp.swapaxes(held[k, i], 0, 1)
             return 0
 
-        lax.fori_loop(0, pairs // 16, turn, 0)
-
-    for k in range(lead):
+        lax.fori_loop(0, groups, turn, 0)
+
+    for k in range(chunks):
+        f_copy(k).start()
+    own_second.start()
+    pl.semaphore_wait(barrier, ncol + ndev - 2)
+    for way, hop, h in pieces:
+        if hop == 1:
+            r_copy(way, 1, h).start()
+    for h in range(2):
+        c_copy(0, 0, h).start()
+    for k in range(chunks):
+        turn_first(k)
+        z_own(k)
+        t_copy(k).start()
+
+    parts_of = {}
+    for number, piece in enumerate(pieces):
+        parts_of.setdefault(min(chunks - 1, (number // 2 + 1) * chunks // 2 - 1), []).append(piece)
+    for k in range(chunks):
         turn_block(k)
-        for piece in by_round[k]:
-            take(*piece)
-        z_round(k)
-    own_first.wait()
+        z_relay(1, k)
+        if k < chunks - 1:
+            for piece in parts_of.get(k, []):
+                take(*piece)
+    late = parts_of.get(chunks - 1, [])
+    for piece in late[:2]:
+        take(*piece)
+    for k in range(min(EARLY, chunks)):
+        for hop in range(2, ndev - 1):
+            z_relay(hop, k)
+    for piece in late[2:]:
+        take(*piece)
     own_second.wait()
     for piece in shared:
         c_arrival(*piece).wait()
@@ -225,7 +238,7 @@
     total[...] = jnp.zeros_like(total)
 
     def one_block(k, _):
-        held = lax.rem(k, lead)
+        z_need(k)
 
         def one_b(b, _):
             left = first_all[pl.ds(k * size, size)].reshape(size * n_a, -1)
@@ -238,26 +251,22 @@
 
         lax.fori_loop(0, n_b // WIDE, one_b, 0)
 
+        @pl.when(k + EARLY < chunks)
+        def _():
+            for hop in range(2, ndev - 1):
+                z_relay(hop, k + EARLY)
+
         def some_c(g, _):
             group = [g * GROUP + i for i in range(GROUP)]
-            left = jnp.concatenate([turned[held, c] for c in group], axis=1)
+            left = jnp.concatenate([held[k, :, c].reshape(pairs, n_d) for c in group], axis=1)
             right = jnp.concatenate([tile[c].reshape(n_b * n_a, n_d) for c in group], axis=1)
             total[...] += lax.dot_general(left, right, NT, preferred_element_type=jnp.float32)
             return 0
 
         lax.fori_loop(0, size // GROUP, some_c, 0)
-
-        @pl.when(k + lead < CHUNKS)
-        def _():
-            turn_block(k + lead)
-
-        @pl.when(((lax.rem(k, 2) == 1) & (k < CHUNKS - 1)) | (k == CHUNKS - 2))
-        def _():
-            z_round(lead + k // 2)
-
         return 0
 
-    lax.fori_loop(0, CHUNKS, one_block, 0)
+    lax.fori_loop(0, chunks, one_block, 0)
 
     some = pairs // ncol
 
@@ -293,11 +302,17 @@
 
     for off in range(1, ndev):
         d_copy(off).start()
+    width = n_a * n_b
+    rows = lax.broadcasted_iota(jnp.int32, (width, width), 0)
+    columns = lax.broadcasted_iota(jnp.int32, (width, width), 1)
+    order = (rows == lax.rem(columns, n_b) * n_a + lax.div(columns, n_b)).astype(jnp.float32)
     result = half_sum[dev]
     for off in range(1, ndev):
         d_copy(off).wait_recv()
         result += final[off]
-    out[...] = result
+    out[...] = jnp.dot(
+        result, order, precision=lax.Precision.HIGHEST, preferred_element_type=jnp.float32
+    )
 
     for off in range(1, ncol):
         s_copy(off).wait_send()
@@ -316,14 +331,16 @@
                     z_copy(way, hop, k).wait_send()
         return 0
 
-    lax.fori_loop(0, CHUNKS, drain, 0)
+    lax.fori_loop(0, chunks, drain, 0)
 
 
 def on_device(ncol, ndev, first_factor, second_factor, amplitudes):
     n_a, n_c, q_first = first_factor.shape
     n_b, n_d, q_second = second_factor.shape
     pairs = amplitudes.shape[0]
-    size = n_c // CHUNKS
+    groups = pairs // BLOCK
+    size = n_a
+    chunks = n_c // size
     far = ncol // 4
     whole = q_first * ndev
     some = pairs // ncol
@@ -331,7 +348,7 @@
     width = n_a * n_b
     anywhere = pl.BlockSpec(memory_space=pl.ANY)
     dma = pltpu.SemaphoreType.DMA
-    got = pl.pallas_call(
+    return pl.pallas_call(
         functools.partial(kernel, ncol, ndev),
         out_shape=jax.ShapeDtypeStruct((few, width), jnp.float32),
         in_specs=[anywhere] * 3,
@@ -339,31 +356,30 @@
         scratch_shapes=[
             pltpu.VMEM((n_c, n_a, whole), jnp.bfloat16),
             pltpu.VMEM((n_b, n_d, whole), jnp.bfloat16),
-            pltpu.VMEM((2, pairs, size, n_d), jnp.bfloat16),
-            pltpu.VMEM((CHUNKS // 2, size, pairs, n_d), jnp.bfloat16),
+            pltpu.VMEM((n_c // BLOCK, groups, BLOCK, BLOCK, n_d), jnp.bfloat16),
             pltpu.VMEM((size, n_b, n_a, n_d), jnp.bfloat16),
             pltpu.VMEM((pairs, width), jnp.float32),
             pltpu.VMEM((ncol, some, width), jnp.float32),
             pltpu.VMEM((ndev, few, width), jnp.float32),
             pltpu.VMEM((ndev, few, width), jnp.float32),
-            dma((2,)),
-            dma((2, ndev - 1, CHUNKS)),
-            dma((2, ndev - 1, CHUNKS)),
+            dma((chunks,)),
+            dma((1,)),
+            dma((2, ndev - 1, chunks)),
+            dma((2, ndev - 1, chunks)),
             dma((2, far, 2)),
             dma((2, far, 2)),
             dma((2, far + 1, 2)),
             dma((2, far + 1, 2)),
-            dma((2,)),
+            dma((n_c // BLOCK,)),
             dma((ncol,)),
             dma((ncol,)),
             dma((ndev,)),
             dma((ndev,)),
         ],
         compiler_params=pltpu.CompilerParams(
-            collective_id=0, has_side_effects=True, vmem_limit_bytes=58 * 2**20
+            collective_id=0, has_side_effects=True, vmem_limit_bytes=67043328
         ),
-    )(jnp.swapaxes(first_factor, 0, 1), second_factor, amplitudes)
-    return jnp.swapaxes(got.reshape(few, n_b, n_a), 1, 2).reshape(few, width)
+    )(first_factor, second_factor, amplitudes.reshape(groups, BLOCK, n_c, n_d))
 
 
 def solution(mesh):

time: 199 us -> 166 us (0.83)
  Pallas kernels: 193 us -> 165 us
  local copies, waits for them, and re-layouts: 5.72 us -> 1.32 us
    pallas_call x1, Pallas kernels: 193 us -> 165 us  [on_device(): pl.pallas_call(functools.partial(kernel, ncol, ndev), out_shape=jax.Shape...]
    unnamed x1, local copies, waits for them, and re-layouts: 4.1 us -> 1.32 us
where the time goes in v1:
time: 166 us
  Pallas kernels  165 us (99%)
    pallas_call x1, Pallas kernels, on_device(): pl.pallas_call(functools.partial(kernel, ncol, ndev), out_shape=jax.Shape...  165 us

profile of v1, /device:TPU:0, one launch (start us, length us, event | category | flops | bytes accessed | tf_op | source)
XLA Modules:
  0.0 166.0 jit_solution(12596487374984112372)
XLA Ops:
  0.0 164.7 %shard_map.37 = f32[16,256]{1,0:T(8,128)} custom-call(bf16[16,128,512]{2,1,0:T(8,128)(2,1)} %first.1, bf16[16,256,256]{2,1,0:T(8,128)(2,1)} %second.1, bf16[32,16,128,256]{3,2,1,0:T(8,128)(2,1)} %bitcast.1), custom_call_target="tpu_custom_call" | custom-call | tf_op jit(solution)/shard_map/pallas_call | solution.py:351
  164.7 1.3 copy.5

commit v2 on v1

--- a/solution.py
+++ b/solution.py
@@ -17,7 +17,7 @@
 
 def kernel(
     ncol, ndev, first, second, amps, out,
-    first_all, second_all, held, tile, total, parts, final, half_sum,
+    first_all, second_all, held, tile, carry, order, total, parts, final, half_sum,
     f_sem, own_sem, z_send, z_recv, r_send, r_recv, c_send, c_recv, t_sem, s_send, s_recv, d_send, d_recv,
 ):
     col, dev = lax.axis_index("col"), lax.axis_index("dev")
@@ -59,9 +59,13 @@
             f_sem.at[k],
         )
 
+    def slot_of(k):
+        return lax.rem(k, chunks - 1)
+
     def t_copy(k):
         return pltpu.make_async_copy(
-            amps.at[:, :, pl.ds(pl.multiple_of(k * BLOCK, BLOCK), BLOCK), :], held.at[k],
+            amps.at[:, :, pl.ds(pl.multiple_of(k * BLOCK, BLOCK), BLOCK), :],
+            held.at[slot_of(k)],
             t_sem.at[k],
         )
 
@@ -106,16 +110,23 @@
             def _():
                 z_copy(way, 1, k).start()
 
-    def z_relay(hop, k):
+    def lone(way):
+        return (dev == 1) if way == 0 else (dev == ndev - 2)
+
+    def z_relay(hop, k, alone=None):
         for way in range(2):
-            @pl.when(receives(way, hop) & sends(way, hop + 1))
+            meant = receives(way, hop) & sends(way, hop + 1)
+            if alone is not None:
+                meant &= lone(way) == alone
+
+            @pl.when(meant)
             def _():
                 z_arrival(way, hop, k).wait()
                 z_copy(way, hop + 1, k).start()
 
-    def z_need(k):
+    def z_need(k, hops):
         for way in range(2):
-            for hop in range(1, ndev):
+            for hop in hops:
                 kept = receives(way, hop)
                 if hop + 1 < ndev:
                     kept &= jnp.logical_not(sends(way, hop + 1))
@@ -193,9 +204,10 @@
 
     def turn_block(k):
         t_copy(k).wait()
+        slot = slot_of(k)
 
         def turn(i, _):
-            held[k, i] = jnp.swapaxes(held[k, i], 0, 1)
+            held[slot, i] = jnp.swapaxes(held[slot, i], 0, 1)
             return 0
 
         lax.fori_loop(0, groups, turn, 0)
@@ -209,115 +221,189 @@
             r_copy(way, 1, h).start()
     for h in range(2):
         c_copy(0, 0, h).start()
+    ahead = chunks - 2
     for k in range(chunks):
         turn_first(k)
-        z_own(k)
+        if k < ahead:
+            z_own(k)
+    for k in range(chunks - 1):
         t_copy(k).start()
 
-    parts_of = {}
-    for number, piece in enumerate(pieces):
-        parts_of.setdefault(min(chunks - 1, (number // 2 + 1) * chunks // 2 - 1), []).append(piece)
-    for k in range(chunks):
+    width = n_a * n_b
+    rows = lax.broadcasted_iota(jnp.int32, (width, width), 0)
+    columns = lax.broadcasted_iota(jnp.int32, (width, width), 1)
+    order[...] = (rows == lax.rem(columns, n_b) * n_a + lax.div(columns, n_b)).astype(jnp.bfloat16)
+
+    def take_hop(want, place):
+        for way in range(2):
+            if place < len(travels(way, want)):
+                take(way, want, travels(way, want)[place])
+
+    def z_relays(k, hops):
+        for hop in hops:
+            z_relay(hop, k, False if hop == 1 else None)
+
+    def z_prompt(blocks):
+        if ndev > 2:
+            for k in blocks:
+                z_relay(1, k, True)
+
+    further = range(2, ndev - 1)
+    for k in range(min(2, chunks - 1)):
         turn_block(k)
-        z_relay(1, k)
-        if k < chunks - 1:
-            for piece in parts_of.get(k, []):
-                take(*piece)
-    late = parts_of.get(chunks - 1, [])
-    for piece in late[:2]:
-        take(*piece)
-    for k in range(min(EARLY, chunks)):
-        for hop in range(2, ndev - 1):
-            z_relay(hop, k)
-    for piece in late[2:]:
-        take(*piece)
+        if ndev > 2:
+            z_relay(1, k)
+        z_own(ahead + k)
+    for k in range(2, chunks - 1):
+        turn_block(k)
+    total[...] = jnp.zeros_like(total)
+    half = 2 + (chunks - 2) // 2
+    take_hop(1, 0)
+    z_prompt(range(2, half))
+    z_relays(0, further)
+    take_hop(1, 1)
+    z_prompt(range(half, chunks))
+    z_relays(1, further)
+    for k in range(2, EARLY):
+        z_relays(k, range(1, ndev - 1))
+    for hop in range(2, far + 1):
+        for place in range(len(travels(0, hop))):
+            take_hop(hop, place)
     own_second.wait()
     for piece in shared:
         c_arrival(*piece).wait()
 
-    total[...] = jnp.zeros_like(total)
+    def rows_of(k):
+        return pl.ds(k * size, size)
+
+    def product(k, b, columns):
+        left = first_all[rows_of(k), :, columns].reshape(size * n_a, -1)
+        right = second_all[pl.ds(b * WIDE, WIDE), :, columns].reshape(WIDE * n_d, -1)
+        return lax.dot_general(left, right, NT, preferred_element_type=jnp.float32)
+
+    def keep(b, got):
+        got = got.astype(jnp.bfloat16)
+        for i in range(WIDE):
+            tile[:, b * WIDE + i] = got[:, i * n_d : (i + 1) * n_d].reshape(size, n_a, n_d)
+
+    def contract(k):
+        slot = slot_of(k)
+
+        def some_c(g, _):
+            group = [g * GROUP + i for i in range(GROUP)]
+            left = jnp.concatenate([held[slot, :, c].reshape(pairs, n_d) for c in group], axis=1)
+            right = jnp.concatenate([tile[c].reshape(n_b * n_a, n_d) for c in group], axis=1)
+            got = lax.dot_general(left, right, NT, preferred_element_type=jnp.float32)
+            total[...] += got.reshape(total.shape)
+            return 0
+
+        lax.fori_loop(0, size // GROUP, some_c, 0)
+
+    everything = pl.ds(0, ndev * q_first)
 
     def one_block(k, _):
-        z_need(k)
+        z_need(k, range(1, ndev))
 
         def one_b(b, _):
-            left = first_all[pl.ds(k * size, size)].reshape(size * n_a, -1)
-            right = second_all[pl.ds(b * WIDE, WIDE)].reshape(WIDE * n_d, -1)
-            got = lax.dot_general(left, right, NT, preferred_element_type=jnp.float32)
-            got = got.astype(jnp.bfloat16)
-            for i in range(WIDE):
-                tile[:, b * WIDE + i] = got[:, i * n_d : (i + 1) * n_d].reshape(size, n_a, n_d)
+            keep(b, product(k, b, everything))
             return 0
 
         lax.fori_loop(0, n_b // WIDE, one_b, 0)
 
         @pl.when(k + EARLY < chunks)
         def _():
-            for hop in range(2, ndev - 1):
-                z_relay(hop, k + EARLY)
-
-        def some_c(g, _):
-            group = [g * GROUP + i for i in range(GROUP)]
-            left = jnp.concatenate([held[k, :, c].reshape(pairs, n_d) for c in group], axis=1)
-            right = jnp.concatenate([tile[c].reshape(n_b * n_a, n_d) for c in group], axis=1)
-            total[...] += lax.dot_general(left, right, NT, preferred_element_type=jnp.float32)
-            return 0
-
-        lax.fori_loop(0, size // GROUP, some_c, 0)
+            z_relays(k + EARLY, range(1, ndev - 1))
+
+        contract(k)
+
+        @pl.when(k == 0)
+        def _():
+            t_copy(chunks - 1).start()
+
+        @pl.when(k == 1)
+        def _():
+            turn_block(chunks - 1)
+
         return 0
 
-    lax.fori_loop(0, chunks, one_block, 0)
-
-    some = pairs // ncol
-
-    def s_copy(off):
-        to = lax.rem(col + off, ncol)
+    lax.fori_loop(0, chunks - 1, one_block, 0)
+
+    end = chunks - 1
+    low = dev * 2 < ndev
+    last = pl.ds(pl.multiple_of(jnp.where(low, ndev - 1, 0) * q_first, q_first), q_first)
+    others = pl.ds(pl.multiple_of(jnp.where(low, 0, q_first), q_first), (ndev - 1) * q_first)
+    z_need(end, range(1, ndev - 1))
+
+    def early_b(b, _):
+        carry[b] = product(end, b, others)
+        return 0
+
+    lax.fori_loop(0, n_b // WIDE, early_b, 0)
+    z_need(end, range(ndev - 1, ndev))
+
+    def late_b(b, _):
+        keep(b, carry[b] + product(end, b, last))
+        return 0
+
+    lax.fori_loop(0, n_b // WIDE, late_b, 0)
+    contract(end)
+
+    targets = [jnp.where(low, ndev - 1 - i, i) for i in range(ndev)]
+
+    def s_copy(off, place):
+        to, target = lax.rem(col + off, ncol), targets[place]
         return pltpu.make_async_remote_copy(
-            src_ref=total.at[pl.ds(pl.multiple_of(to * some, some), some)],
-            dst_ref=parts.at[off],
-            send_sem=s_send.at[off],
-            recv_sem=s_recv.at[off],
+            src_ref=total.at[to, target],
+            dst_ref=parts.at[off, target],
+            send_sem=s_send.at[off, place],
+            recv_sem=s_recv.at[off, place],
             device_id={"col": to},
             device_id_type=MESH,
         )
 
-    for off in range(1, ncol):
-        s_copy(off).start()
-    mine = total[pl.ds(pl.multiple_of(col * some, some), some), :]
-    for off in range(1, ncol):
-        s_copy(off).wait_recv()
-        mine += parts[off]
-    half_sum[...] = mine.reshape(half_sum.shape)
-
-    def d_copy(off):
-        to = lax.rem(dev + off, ndev)
+    def d_copy(target):
         return pltpu.make_async_remote_copy(
-            src_ref=half_sum.at[to],
-            dst_ref=final.at[off],
-            send_sem=d_send.at[off],
-            recv_sem=d_recv.at[off],
-            device_id={"dev": to},
+            src_ref=half_sum.at[target],
+            dst_ref=final.at[dev],
+            send_sem=d_send.at[target],
+            recv_sem=d_recv.at[dev],
+            device_id={"dev": target},
             device_id_type=MESH,
         )
 
-    for off in range(1, ndev):
-        d_copy(off).start()
-    width = n_a * n_b
-    rows = lax.broadcasted_iota(jnp.int32, (width, width), 0)
-    columns = lax.broadcasted_iota(jnp.int32, (width, width), 1)
-    order = (rows == lax.rem(columns, n_b) * n_a + lax.div(columns, n_b)).astype(jnp.float32)
+    for place in range(ndev):
+        for off in range(1, ncol):
+            s_copy(off, place).start()
+    for place in range(ndev):
+        target = targets[place]
+        mine = total[col, target]
+        for off in range(1, ncol):
+            s_copy(off, place).wait_recv()
+            mine += parts[off, target]
+        half_sum[target] = mine
+
+        @pl.when(target != dev)
+        def _():
+            d_copy(target).start()
+
     result = half_sum[dev]
     for off in range(1, ndev):
-        d_copy(off).wait_recv()
-        result += final[off]
-    out[...] = jnp.dot(
-        result, order, precision=lax.Precision.HIGHEST, preferred_element_type=jnp.float32
-    )
-
-    for off in range(1, ncol):
-        s_copy(off).wait_send()
+        source = lax.rem(dev + off, ndev)
+        pltpu.make_async_copy(final.at[source], final.at[source], d_recv.at[source]).wait()
+        result += final[source]
+    high = result.astype(jnp.bfloat16)
+    result -= high.astype(jnp.float32)
+    middle = result.astype(jnp.bfloat16)
+    result -= middle.astype(jnp.float32)
+    split = (high, middle, result.astype(jnp.bfloat16))
+    moved = [jnp.dot(part, order[...], preferred_element_type=jnp.float32) for part in split]
+    out[...] = moved[0] + moved[1] + moved[2]
+
+    for place in range(ndev):
+        for off in range(1, ncol):
+            s_copy(off, place).wait_send()
     for off in range(1, ndev):
-        d_copy(off).wait_send()
+        d_copy(lax.rem(dev + off, ndev)).wait_send()
     for piece in pieces:
         r_copy(*piece).wait_send()
     for piece in shared:
@@ -356,10 +442,12 @@
         scratch_shapes=[
             pltpu.VMEM((n_c, n_a, whole), jnp.bfloat16),
             pltpu.VMEM((n_b, n_d, whole), jnp.bfloat16),
-            pltpu.VMEM((n_c // BLOCK, groups, BLOCK, BLOCK, n_d), jnp.bfloat16),
+            pltpu.VMEM((n_c // BLOCK - 1, groups, BLOCK, BLOCK, n_d), jnp.bfloat16),
             pltpu.VMEM((size, n_b, n_a, n_d), jnp.bfloat16),
-            pltpu.VMEM((pairs, width), jnp.float32),
-            pltpu.VMEM((ncol, some, width), jnp.float32),
+            pltpu.VMEM((n_b // WIDE, size * n_a, WIDE * n_d), jnp.float32),
+            pltpu.VMEM((width, width), jnp.bfloat16),
+            pltpu.VMEM((ncol, ndev, few, width), jnp.float32),
+            pltpu.VMEM((ncol, ndev, few, width), jnp.float32),
             pltpu.VMEM((ndev, few, width), jnp.float32),
             pltpu.VMEM((ndev, few, width), jnp.float32),
             dma((chunks,)),
@@ -371,8 +459,8 @@
             dma((2, far + 1, 2)),
             dma((2, far + 1, 2)),
             dma((n_c // BLOCK,)),
-            dma((ncol,)),
-            dma((ncol,)),
+            dma((ncol, ndev)),
+            dma((ncol, ndev)),
             dma((ndev,)),
             dma((ndev,)),
         ],

time: 166 us -> 157 us (0.946)
  Pallas kernels: 165 us -> 156 us
    pallas_call x1, Pallas kernels: 165 us -> 156 us  [on_device(): pl.pallas_call(functools.partial(kernel, ncol, ndev), out_shape=jax.Shape...]
where the time goes in v2:
time: 157 us
  Pallas kernels  156 us (99%)
    pallas_call x1, Pallas kernels, on_device(): pl.pallas_call(functools.partial(kernel, ncol, ndev), out_shape=jax.Shape...  156 us

profile of v2, /device:TPU:0, one launch (start us, length us, event | category | flops | bytes accessed | tf_op | source)
XLA Modules:
  0.0 156.9 jit_solution(5295413753587048725)
XLA Ops:
  0.0 155.6 %shard_map.37 = f32[16,256]{1,0:T(8,128)} custom-call(bf16[16,128,512]{2,1,0:T(8,128)(2,1)} %first.1, bf16[16,256,256]{2,1,0:T(8,128)(2,1)} %second.1, bf16[32,16,128,256]{3,2,1,0:T(8,128)(2,1)} %bitcast.1), custom_call_target="tpu_custom_call" | custom-call | tf_op jit(solution)/shard_map/pallas_call | solution.py:437
  155.6 1.3 copy.5

commit v3 on v2

--- a/solution.py
+++ b/solution.py
@@ -17,8 +17,8 @@
 
 def kernel(
     ncol, ndev, first, second, amps, out,
-    first_all, second_all, held, tile, carry, order, total, parts, final, half_sum,
-    f_sem, own_sem, z_send, z_recv, r_send, r_recv, c_send, c_recv, t_sem, s_send, s_recv, d_send, d_recv,
+    first_all, second_all, held, tile, carry, order, total, mate, joined, parts, final, half_sum,
+    f_sem, own_sem, z_send, z_recv, r_send, r_recv, c_send, c_recv, t_sem, x_send, x_recv, s_send, s_recv, d_send, d_recv,
 ):
     col, dev = lax.axis_index("col"), lax.axis_index("dev")
     n_a, n_c, q_first = first.shape
@@ -74,27 +74,39 @@
         own_sem.at[0],
     )
 
-    def z_slice(source, k):
-        return first_all.at[
-            pl.ds(k * size, size), :, pl.ds(pl.multiple_of(source * q_first, q_first), q_first)
+    def z_slice(source, k, share, shares):
+        wide = q_first // shares
+        start = pl.multiple_of(source * q_first + share * wide, wide)
+        return first_all.at[pl.ds(k * size, size), :, pl.ds(start, wide)]
+
+    def shares_of(hop):
+        return 2 if hop == ndev - 1 else 1
+
+    def z_copies(way, hop, k):
+        step = 1 if way == 0 else -1
+        source, shares = dev - step * (hop - 1), shares_of(hop)
+        return [
+            pltpu.make_async_remote_copy(
+                src_ref=z_slice(source, k, share, shares),
+                dst_ref=z_slice(source, k, share, shares),
+                send_sem=z_send.at[way, hop - 1, k, share],
+                recv_sem=z_recv.at[way, hop - 1, k, share],
+                device_id={"dev": dev + step},
+                device_id_type=MESH,
+            )
+            for share in range(shares)
         ]
 
-    def z_copy(way, hop, k):
+    def z_arrivals(way, hop, k, chosen=(0, 1)):
         step = 1 if way == 0 else -1
-        here = z_slice(dev - step * (hop - 1), k)
-        return pltpu.make_async_remote_copy(
-            src_ref=here,
-            dst_ref=here,
-            send_sem=z_send.at[way, hop - 1, k],
-            recv_sem=z_recv.at[way, hop - 1, k],
-            device_id={"dev": dev + step},
-            device_id_type=MESH,
-        )
-
-    def z_arrival(way, hop, k):
-        step = 1 if way == 0 else -1
-        here = z_slice(dev - step * hop, k)
-        return pltpu.make_async_copy(here, here, z_recv.at[way, hop - 1, k])
+        source, shares = dev - step * hop, shares_of(hop)
+        here = {
+            share: z_slice(source, k, share, shares) for share in range(shares) if share in chosen
+        }
+        return [
+            pltpu.make_async_copy(ref, ref, z_recv.at[way, hop - 1, k, share])
+            for share, ref in here.items()
+        ]
 
     def sends(way, hop):
         if way == 0:
@@ -108,7 +120,8 @@
         for way in range(2):
             @pl.when(sends(way, 1))
             def _():
-                z_copy(way, 1, k).start()
+                for copy in z_copies(way, 1, k):
+                    copy.start()
 
     def lone(way):
         return (dev == 1) if way == 0 else (dev == ndev - 2)
@@ -121,10 +134,12 @@
 
             @pl.when(meant)
             def _():
-                z_arrival(way, hop, k).wait()
-                z_copy(way, hop + 1, k).start()
-
-    def z_need(k, hops):
+                for arrival in z_arrivals(way, hop, k):
+                    arrival.wait()
+                for copy in z_copies(way, hop + 1, k):
+                    copy.start()
+
+    def z_need(k, hops, shares=(0, 1)):
         for way in range(2):
             for hop in hops:
                 kept = receives(way, hop)
@@ -133,7 +148,8 @@
 
                 @pl.when(kept)
                 def _():
-                    z_arrival(way, hop, k).wait()
+                    for arrival in z_arrivals(way, hop, k, shares):
+                        arrival.wait()
 
     wide = n_b // 2
 
@@ -330,7 +346,12 @@
 
     end = chunks - 1
     low = dev * 2 < ndev
-    last = pl.ds(pl.multiple_of(jnp.where(low, ndev - 1, 0) * q_first, q_first), q_first)
+    piece_q = q_first // 2
+
+    def last_q(share):
+        start = jnp.where(low, ndev - 1, 0) * q_first + share * piece_q
+        return pl.ds(pl.multiple_of(start, piece_q), piece_q)
+
     others = pl.ds(pl.multiple_of(jnp.where(low, 0, q_first), q_first), (ndev - 1) * q_first)
     z_need(end, range(1, ndev - 1))
 
@@ -339,25 +360,63 @@
         return 0
 
     lax.fori_loop(0, n_b // WIDE, early_b, 0)
-    z_need(end, range(ndev - 1, ndev))
+    z_need(end, range(ndev - 1, ndev), (0,))
+
+    def middle_b(b, _):
+        carry[b] += product(end, b, last_q(0))
+        return 0
+
+    lax.fori_loop(0, n_b // WIDE, middle_b, 0)
+    z_need(end, range(ndev - 1, ndev), (1,))
 
     def late_b(b, _):
-        keep(b, carry[b] + product(end, b, last))
+        keep(b, carry[b] + product(end, b, last_q(1)))
         return 0
 
     lax.fori_loop(0, n_b // WIDE, late_b, 0)
-    contract(end)
 
     targets = [jnp.where(low, ndev - 1 - i, i) for i in range(ndev)]
+    per_chip = groups // chips
+    per_core = per_chip // 2
+
+    def contract_side(side):
+        slot = slot_of(end)
+
+        def some_c(g, _):
+            group = [g * GROUP + i for i in range(GROUP)]
+            left = jnp.concatenate([
+                jnp.concatenate([
+                    held[slot, pl.ds(i * per_chip + side * per_core, per_core), c].reshape(-1, n_d)
+                    for i in range(chips)
+                ], axis=0)
+                for c in group
+            ], axis=1)
+            right = jnp.concatenate([tile[c].reshape(n_b * n_a, n_d) for c in group], axis=1)
+            got = lax.dot_general(left, right, NT, preferred_element_type=jnp.float32)
+            total[:, side] += got.reshape(mate.shape)
+            return 0
+
+        lax.fori_loop(0, size // GROUP, some_c, 0)
+
+    def x_copy(place):
+        target = targets[place]
+        return pltpu.make_async_remote_copy(
+            src_ref=total.at[:, 1 - core, target],
+            dst_ref=mate.at[:, target],
+            send_sem=x_send.at[place],
+            recv_sem=x_recv.at[place],
+            device_id={"col": partner},
+            device_id_type=MESH,
+        )
 
     def s_copy(off, place):
-        to, target = lax.rem(col + off, ncol), targets[place]
+        to, target = lax.rem(chip + off, chips), targets[place]
         return pltpu.make_async_remote_copy(
-            src_ref=total.at[to, target],
+            src_ref=joined.at[to, target],
             dst_ref=parts.at[off, target],
             send_sem=s_send.at[off, place],
             recv_sem=s_recv.at[off, place],
-            device_id={"col": to},
+            device_id={"col": to * 2 + core},
             device_id_type=MESH,
         )
 
@@ -371,13 +430,36 @@
             device_id_type=MESH,
         )
 
+    contract_side(1 - core)
     for place in range(ndev):
-        for off in range(1, ncol):
-            s_copy(off, place).start()
+        x_copy(place).start()
+    contract_side(core)
     for place in range(ndev):
         target = targets[place]
-        mine = total[col, target]
-        for off in range(1, ncol):
+        x_copy(place).wait_recv()
+        joined[:, target] = total[:, core, target] + mate[:, target]
+        for off in range(1, chips):
+            s_copy(off, place).start()
+    for piece in pieces:
+        r_copy(*piece).wait_send()
+    for piece in shared:
+        c_copy(*piece).wait_send()
+
+    def drain(k, _):
+        for way in range(2):
+            for hop in range(1, ndev):
+                @pl.when(sends(way, hop))
+                def _():
+                    for copy in z_copies(way, hop, k):
+                        copy.wait_send()
+        return 0
+
+    lax.fori_loop(0, chunks, drain, 0)
+
+    for place in range(ndev):
+        target = targets[place]
+        mine = joined[chip, target]
+        for off in range(1, chips):
             s_copy(off, place).wait_recv()
             mine += parts[off, target]
         half_sum[target] = mine
@@ -400,24 +482,11 @@
     out[...] = moved[0] + moved[1] + moved[2]
 
     for place in range(ndev):
-        for off in range(1, ncol):
+        x_copy(place).wait_send()
+        for off in range(1, chips):
             s_copy(off, place).wait_send()
     for off in range(1, ndev):
         d_copy(lax.rem(dev + off, ndev)).wait_send()
-    for piece in pieces:
-        r_copy(*piece).wait_send()
-    for piece in shared:
-        c_copy(*piece).wait_send()
-
-    def drain(k, _):
-        for way in range(2):
-            for hop in range(1, ndev):
-                @pl.when(sends(way, hop))
-                def _():
-                    z_copy(way, hop, k).wait_send()
-        return 0
-
-    lax.fori_loop(0, chunks, drain, 0)
 
 
 def on_device(ncol, ndev, first_factor, second_factor, amplitudes):
@@ -427,7 +496,8 @@
     groups = pairs // BLOCK
     size = n_a
     chunks = n_c // size
-    far = ncol // 4
+    chips = ncol // 2
+    far = chips // 2
     whole = q_first * ndev
     some = pairs // ncol
     few = some // ndev
@@ -446,21 +516,25 @@
             pltpu.VMEM((size, n_b, n_a, n_d), jnp.bfloat16),
             pltpu.VMEM((n_b // WIDE, size * n_a, WIDE * n_d), jnp.float32),
             pltpu.VMEM((width, width), jnp.bfloat16),
-            pltpu.VMEM((ncol, ndev, few, width), jnp.float32),
-            pltpu.VMEM((ncol, ndev, few, width), jnp.float32),
+            pltpu.VMEM((chips, 2, ndev, few, width), jnp.float32),
+            pltpu.VMEM((chips, ndev, few, width), jnp.float32),
+            pltpu.VMEM((chips, ndev, few, width), jnp.float32),
+            pltpu.VMEM((chips, ndev, few, width), jnp.float32),
             pltpu.VMEM((ndev, few, width), jnp.float32),
             pltpu.VMEM((ndev, few, width), jnp.float32),
             dma((chunks,)),
             dma((1,)),
-            dma((2, ndev - 1, chunks)),
-            dma((2, ndev - 1, chunks)),
+            dma((2, ndev - 1, chunks, 2)),
+            dma((2, ndev - 1, chunks, 2)),
             dma((2, far, 2)),
             dma((2, far, 2)),
             dma((2, far + 1, 2)),
             dma((2, far + 1, 2)),
             dma((n_c // BLOCK,)),
-            dma((ncol, ndev)),
-            dma((ncol, ndev)),
+            dma((ndev,)),
+            dma((ndev,)),
+            dma((chips, ndev)),
+            dma((chips, ndev)),
             dma((ndev,)),
             dma((ndev,)),
         ],

time: 157 us -> 157 us (level)
  no operation moved by 1% of the time
where the time goes in v3:
time: 157 us; the launch traced here: 156 us
  Pallas kernels  155 us (99%)
    pallas_call x1, Pallas kernels, on_device(): pl.pallas_call(functools.partial(kernel, ncol, ndev), out_shape=jax.Shape...  155 us

profile of v3, /device:TPU:0, one launch (start us, length us, event | category | flops | bytes accessed | tf_op | source)
XLA Modules:
  0.0 156.3 jit_solution(3858536901184033442)
XLA Ops:
  0.0 155.0 %shard_map.37 = f32[16,256]{1,0:T(8,128)} custom-call(bf16[16,128,512]{2,1,0:T(8,128)(2,1)} %first.1, bf16[16,256,256]{2,1,0:T(8,128)(2,1)} %second.1, bf16[32,16,128,256]{3,2,1,0:T(8,128)(2,1)} %bitcast.1), custom_call_target="tpu_custom_call" | custom-call | tf_op jit(solution)/shard_map/pallas_call | solution.py:507
  155.0 1.3 copy.5
